TPU v7x, 32 devices: a whole 2x2x4 slice. The times are simulated.
32 devices in a mesh: tok: 4 (over y, core), feat: 8 (over z, x).
Axes of the slice: x: 2, y: 2, z: 4, core: 2. Of those that a mesh axis runs over, the one named last changes fastest.
Arguments:
- tokens: bfloat16 [4096, 2048], P('tok', 'feat'), may hold values from -6 to 6
- level_bits: int32 [2, 4], replicated, may hold values from 0 to 3, each once within a row
- up_blocks: bfloat16 [2, 16, 5, 128, 512], P(None, 'feat', None, None, 'tok'), may hold values from -0.21875 to 0.21875
- down_blocks: bfloat16 [2, 16, 5, 512, 128], P(None, 'feat', None, None, 'tok'), may hold values from -0.109375 to 0.109375
- rank_in: bfloat16 [2, 2048, 256], replicated, may hold values from -0.125 to 0.125
- rank_up: bfloat16 [2, 256, 8192], P(None, None, 'feat'), may hold values from -0.15625 to 0.15625
- rank_down: bfloat16 [2, 8192, 256], P(None, 'feat'), may hold values from -0.0625 to 0.0625
- rank_out: bfloat16 [2, 256, 2048], P(None, None, 'feat'), may hold values from -0.15625 to 0.15625
Outputs:
- outputs: bfloat16 [4096, 2048], P('tok', 'feat')
Inputs may be any that keep to these rules, and one draw needn't show every extreme that they name: `level_bits`: each row is a permutation of the bits 0 to 3.
All inputs are finite; a program needn't handle non-finite values.
Results may differ from a plain program's by a relative error of at most 0.015.
Values may be sent and summed in bfloat16 or wider, within the bound.
A program may use at most 64 MiB of HBM per device.

v0:
```python
import functools
import math

import jax
import jax.numpy as jnp
from jax import lax
from jax.experimental import pallas as pl
from jax.experimental.pallas import tpu as pltpu
from jax.sharding import PartitionSpec as P

CHUNK_ROWS = 256
SKEW = 1
LATER = 1
MESH = pl.DeviceIdType.MESH


def bits_of(count):
    return count.bit_length() - 1


def network(cfg, tokens, level_bits, up_in, down_in, rank_in, rank_up, rank_down, rank_out, out, *scratch):
    (xbuf, xrecv, tsend, trecv, part, half, full, hid, acc, wup, wdown) = scratch[:11]
    rest = scratch[11:]
    layers, rows, width = cfg["layers"], cfg["rows"], cfg["width"]
    blocks, wb, hb = cfg["blocks"], cfg["wb"], cfg["hb"]
    n_feat, n_tok, rank = cfg["n_feat"], cfg["n_tok"], cfg["rank"]
    cr = cfg["chunk"]
    chunks = rows // cr
    local_bits = bits_of(blocks)
    nb = bits_of(n_feat)
    levels = local_bits + nb
    gather = cfg["gather"]
    if gather:
        upg, downg = rest[:layers], rest[layers : 2 * layers]
        wsend, wrecv, wloc = rest[2 * layers : 2 * layers + 3]
        rest = rest[2 * layers + 3 :]
    else:
        upg = [up_in.at[l] for l in range(layers)]
        downg = [down_in.at[l] for l in range(layers)]
    xs_sem, xr_sem, ts_sem, tr_sem, as_sem, ar_sem = rest

    me = lax.axis_index("feat")
    me_tok = lax.axis_index("tok")
    mybit = [(me // (1 << b)) % 2 for b in range(nb)]
    partner = [me + (1 << b) * (1 - 2 * mybit[b]) for b in range(nb)]

    barrier = pltpu.get_barrier_semaphore()
    for b in range(nb):
        pl.semaphore_signal(barrier, inc=1, device_id={"feat": partner[b]}, device_id_type=MESH)
    greeted = nb
    if gather:
        for o in range(1, n_tok):
            pl.semaphore_signal(
                barrier, inc=1, device_id={"tok": lax.rem(me_tok + o, n_tok)}, device_id_type=MESH
            )
        greeted += n_tok - 1
    pl.semaphore_wait(barrier, greeted)

    def weight_copy(l, kind, o):
        if kind == 0:
            cols = up_in.shape[-1]
            src = up_in.at[l]
            dst = upg[l].at[:, :, :, pl.ds(pl.multiple_of(me_tok * cols, cols), cols)]
        else:
            cols = down_in.shape[-2]
            src = down_in.at[l]
            dst = downg[l].at[:, :, pl.ds(pl.multiple_of(me_tok * cols, cols), cols), :]
        if o == 0:
            return pltpu.make_async_copy(src, dst, wloc.at[l, kind])
        return pltpu.make_async_remote_copy(
            src_ref=src,
            dst_ref=dst,
            send_sem=wsend.at[l, kind, o - 1],
            recv_sem=wrecv.at[l, kind, o - 1],
            device_id={"tok": lax.rem(me_tok + o, n_tok)},
            device_id_type=MESH,
        )

    def start_weights():
        for l in range(layers):
            for kind in range(2):
                for o in range(n_tok):
                    weight_copy(l, kind, o).start()

    prepared = set()

    def prepare(l, kind):
        if (l, kind) in prepared:
            return
        prepared.add((l, kind))
        if gather:
            for o in range(n_tok):
                copy = weight_copy(l, kind, o)
                copy.wait() if o == 0 else copy.wait_recv()
        order = []
        for b in range(levels):
            at = 0
            for k in range(levels):
                at = jnp.maximum(at, jnp.where(level_bits[l, k] == b, 1 + k, 0))
            order.append(at)
        for j in range(blocks):
            if kind == 0:
                wup[l, j, pl.ds(0, wb), :] = upg[l][j, 0]
                for b in range(levels):
                    wup[l, j, pl.ds((1 + b) * wb, wb), :] = upg[l][j, order[b]]
                wup[l, j, pl.ds((1 + levels) * wb, rank), :] = rank_up[l, :, pl.ds(j * hb, hb)]
            else:
                wdown[l, j, pl.ds(0, wb), :] = downg[l][j, 0]
                for b in range(levels):
                    wdown[l, j, pl.ds((1 + b) * wb, wb), :] = downg[l][j, order[b]]

    def x_copy(l, c, b):
        at = pl.ds(c * cr, cr)
        return pltpu.make_async_remote_copy(
            src_ref=xbuf.at[l, at, :],
            dst_ref=xrecv.at[l, b, at, :],
            send_sem=xs_sem.at[l, c, b],
            recv_sem=xr_sem.at[l, c, b],
            device_id={"feat": partner[b]},
            device_id_type=MESH,
        )

    def t_copy(l, c, b):
        at = pl.ds(c * cr, cr)
        return pltpu.make_async_remote_copy(
            src_ref=tsend.at[l, b, at, :],
            dst_ref=trecv.at[l, b, at, :],
            send_sem=ts_sem.at[l, c, b],
            recv_sem=tr_sem.at[l, c, b],
            device_id={"feat": partner[b]},
            device_id_type=MESH,
        )

    last = nb - 1
    sizes = [cr >> (k + 1) for k in range(last)]
    own_at = [0]
    for k in range(last):
        own_at.append(own_at[-1] + mybit[k] * sizes[k])
    away_at = [own_at[k] + (1 - mybit[k]) * sizes[k] for k in range(last)]
    piece = cr >> last
    half_at = [sum(sizes[:k]) for k in range(last + 1)]
    half_rows = half_at[-1] + piece

    def reduce_copy(u, c, k):
        if k < last:
            src = part.at[u, pl.ds(pl.multiple_of(c * cr + away_at[k], sizes[k]), sizes[k]), :]
            size = sizes[k]
        else:
            src = part.at[u, pl.ds(pl.multiple_of(c * cr + own_at[last], piece), piece), :]
            size = piece
        return pltpu.make_async_remote_copy(
            src_ref=src,
            dst_ref=half.at[u, pl.ds(c * half_rows + half_at[k], size), :],
            send_sem=as_sem.at[u, c, k],
            recv_sem=ar_sem.at[u, c, k],
            device_id={"feat": partner[k]},
            device_id_type=MESH,
        )

    def spread_copy(u, c, k):
        size = cr >> (k + 1)
        at = pl.ds(pl.multiple_of(c * cr + own_at[k + 1], size), size)
        return pltpu.make_async_remote_copy(
            src_ref=full.at[u, at, :],
            dst_ref=full.at[u, at, :],
            send_sem=as_sem.at[u, c, nb + k],
            recv_sem=ar_sem.at[u, c, nb + k],
            device_id={"feat": partner[k]},
            device_id_type=MESH,
        )

    def start_bulk(u, c, stage):
        for b in reversed(range(nb)):
            if min(LATER, nb) * (0 if b == last else 1) == stage:
                (t_copy if u % 2 else x_copy)(u // 2, c, b).start()

    def sum_stage(u, c, k):
        reduce_copy(u, c, k).wait_recv()
        size = sizes[k] if k < last else piece
        start = own_at[k + 1] if k < last else own_at[last]
        at = pl.ds(pl.multiple_of(c * cr + start, size), size)
        total = part[u, at, :].astype(jnp.float32) + half[
            u, pl.ds(c * half_rows + half_at[k], size), :
        ].astype(jnp.float32)
        if k < last:
            part[u, at, :] = total.astype(jnp.bfloat16)
            reduce_copy(u, c, k + 1).start()
        else:
            full[u, at, :] = total.astype(jnp.bfloat16)
            if last > 0:
                spread_copy(u, c, last - 1).start()
        start_bulk(u, c, k + 1)

    def spread_stage(u, c, k):
        spread_copy(u, c, k).wait_recv()
        if k > 0:
            spread_copy(u, c, k - 1).start()

    def sum_stages(u, c):
        found = [functools.partial(sum_stage, u, c, k) for k in range(nb)]
        for k in range(last - 1, 0, -1):
            found.append(functools.partial(spread_stage, u, c, k))
        return found

    def finish_sum(u, c):
        if last > 0:
            spread_stage(u, c, 0)

    def begin(l, c):
        at = pl.ds(c * cr, cr)
        u = 2 * l
        x = xbuf[l, at, :]
        mine = rank_in[l, pl.ds(pl.multiple_of(me * width, width), width), :]
        part[u, at, :] = jnp.dot(x, mine, preferred_element_type=jnp.float32).astype(jnp.bfloat16)
        reduce_copy(u, c, 0).start()
        start_bulk(u, c, 0)

    def first(c):
        at = pl.ds(c * cr, cr)
        xbuf[0, at, :] = tokens[at, :]
        begin(0, c)

    def middle(l, c):
        at = pl.ds(c * cr, cr)
        u = 2 * l + 1
        prepare(l, 0)
        finish_sum(u - 1, c)
        for b in range(nb):
            x_copy(l, c, b).wait_recv()
        for j in range(blocks):
            pieces = [xbuf[l, at, pl.ds(j * wb, wb)]]
            for b in range(local_bits):
                pieces.append(xbuf[l, at, pl.ds((j ^ (1 << b)) * wb, wb)])
            for b in range(nb):
                pieces.append(xrecv[l, b, at, pl.ds(j * wb, wb)])
            pieces.append(full[u - 1, at, :])
            pre = jnp.dot(
                jnp.concatenate(pieces, axis=1), wup[l, j], preferred_element_type=jnp.float32
            )
            act = 0.5 * pre * (1.0 + lax.erf(pre * (1.0 / math.sqrt(2.0))))
            hid[at, pl.ds(j * hb, hb)] = act.astype(jnp.bfloat16)
        part[u, at, :] = jnp.dot(
            hid[at, :], rank_down[l], preferred_element_type=jnp.float32
        ).astype(jnp.bfloat16)
        reduce_copy(u, c, 0).start()
        prepare(l, 1)
        own = [None] * blocks
        for j in range(blocks):
            out_j = lax.dot_general(
                hid[at, pl.ds(j * hb, hb)],
                wdown[l, j],
                (((1,), (1,)), ((), ())),
                preferred_element_type=jnp.float32,
            )
            terms = [out_j[:, k * wb : (k + 1) * wb] for k in range(1 + levels)]
            for b in range(nb):
                tsend[l, b, at, pl.ds(j * wb, wb)] = terms[1 + local_bits + b].astype(jnp.bfloat16)
            for to, value in [(j, terms[0])] + [(j ^ (1 << b), terms[1 + b]) for b in range(local_bits)]:
                own[to] = value if own[to] is None else own[to] + value
        start_bulk(u, c, 0)
        for j in range(blocks):
            col = pl.ds(j * wb, wb)
            acc[at, col] = own[j] + xbuf[l, at, col].astype(jnp.float32)

    def close(l, c):
        at = pl.ds(c * cr, cr)
        u = 2 * l + 1
        finish_sum(u, c)
        total = acc[at, :] + jnp.dot(full[u, at, :], rank_out[l], preferred_element_type=jnp.float32)
        for b in range(nb):
            t_copy(l, c, b).wait_recv()
            total = total + trecv[l, b, at, :].astype(jnp.float32)
        result = total.astype(jnp.bfloat16)
        if l + 1 < layers:
            xbuf[l + 1, at, :] = result
            begin(l + 1, c)
        else:
            out[at, :] = result

    plan = []
    for c in range(chunks):
        steps = [functools.partial(first, c)]
        for l in range(layers):
            steps += sum_stages(2 * l, c)
            steps.append(functools.partial(middle, l, c))
            steps += sum_stages(2 * l + 1, c)
            steps.append(functools.partial(close, l, c))
        plan.append(steps)

    plan[0][0]()
    if gather:
        start_weights()
    for tick in range(1, len(plan[0]) + cfg["skew"] * (chunks - 1)):
        for c in range(chunks):
            at = tick - cfg["skew"] * c
            if 0 <= at < len(plan[c]):
                plan[c][at]()

    for l in range(layers):
        if gather:
            for kind in range(2):
                for o in range(1, n_tok):
                    weight_copy(l, kind, o).wait_send()
        for c in range(chunks):
            for b in range(nb):
                x_copy(l, c, b).wait_send()
                t_copy(l, c, b).wait_send()
            for u in (2 * l, 2 * l + 1):
                for k in range(nb):
                    reduce_copy(u, c, k).wait_send()
                for k in range(last):
                    spread_copy(u, c, k).wait_send()


def per_device(tokens, level_bits, up_blocks, down_blocks, rank_in, rank_up, rank_down, rank_out):
    rows, width = tokens.shape
    layers, blocks, parts, wb, up_cols = up_blocks.shape
    hb, down_cols = down_blocks.shape[3:]
    n_tok, n_feat = lax.axis_size("tok"), lax.axis_size("feat")
    rank = rank_in.shape[-1]
    hidden = blocks * hb
    nb = bits_of(n_feat)
    chunk = min(CHUNK_ROWS, rows)
    chunks = rows // chunk
    gather = n_tok > 1 and up_cols % 128 == 0 and down_cols % 16 == 0
    if not gather:
        up_blocks = lax.all_gather(up_blocks, "tok", axis=4, tiled=True)
        down_blocks = lax.all_gather(down_blocks, "tok", axis=4, tiled=True)
    down_blocks = jnp.swapaxes(down_blocks, 3, 4)
    cfg = dict(
        layers=layers, rows=rows, width=width, blocks=blocks, wb=wb, hb=hb, n_feat=n_feat,
        n_tok=n_tok, rank=rank, chunk=chunk, gather=gather, skew=SKEW,
    )
    bf16 = jnp.bfloat16
    uses = 2 * layers
    half_rows = chunk
    scratch = [
        pltpu.VMEM((layers, rows, width), bf16),
        pltpu.VMEM((layers, nb, rows, width), bf16),
        pltpu.VMEM((layers, nb, rows, width), bf16),
        pltpu.VMEM((layers, nb, rows, width), bf16),
        pltpu.VMEM((uses, rows, rank), bf16),
        pltpu.VMEM((uses, chunks * half_rows, rank), bf16),
        pltpu.VMEM((uses, rows, rank), bf16),
        pltpu.VMEM((rows, hidden), bf16),
        pltpu.VMEM((rows, width), jnp.float32),
        pltpu.VMEM((layers, blocks, parts * wb + rank, hb), bf16),
        pltpu.VMEM((layers, blocks, parts * wb, hb), bf16),
    ]
    dma = pltpu.SemaphoreType.DMA
    if gather:
        scratch += [pltpu.VMEM((blocks, parts, wb, hb), bf16)] * (2 * layers)
        scratch += [
            dma((layers, 2, n_tok - 1)),
            dma((layers, 2, n_tok - 1)),
            dma((layers, 2)),
        ]
    scratch += [dma((layers, chunks, nb))] * 4 + [dma((uses, chunks, 2 * nb - 1))] * 2
    vmem = pl.BlockSpec(memory_space=pltpu.VMEM)
    smem = pl.BlockSpec(memory_space=pltpu.SMEM)
    return pl.pallas_call(
        functools.partial(network, cfg),
        out_shape=jax.ShapeDtypeStruct((rows, width), bf16),
        in_specs=[vmem, smem] + [vmem] * 6,
        out_specs=vmem,
        scratch_shapes=scratch,
        compiler_params=pltpu.CompilerParams(
            collective_id=0, has_side_effects=True, vmem_limit_bytes=63 * 1024 * 1024
        ),
    )(tokens, level_bits, up_blocks, down_blocks, rank_in, rank_up, rank_down, rank_out)


def solution(mesh):
    return jax.shard_map(
        per_device,
        mesh=mesh,
        in_specs=(
            P("tok", "feat"),
            P(),
            P(None, "feat", None, None, "tok"),
            P(None, "feat", None, None, "tok"),
            P(),
            P(None, None, "feat"),
            P(None, "feat", None),
            P(None, None, "feat"),
        ),
        out_specs=P("tok", "feat"),
        check_vma=False,
    )
```

profile of v0, /device:TPU:0, one launch (start us, length us, event | category | flops | bytes accessed | tf_op | source)
XLA Modules:
  0.0 146.3 jit_solution(15288670204581476173)
XLA Ops:
  0.0 144.5 %shard_map.82 = bf16[1024,256]{1,0:T(8,128)(2,1)} custom-call(bf16[1024,256]{1,0:T(8,128)(2,1)} %tokens.1, s32[2,4]{1,0:T(2,128)} %level_bits.1, bf16[2,2,5,128,128]{4,3,2,1,0:T(8,128)(2,1)} %up_in.1, bf16[2,2,5,32,512]{4,3,2,1,0:T(8,128)(2,1)} %bitcast.1, bf16[2,2048,256]{2,1,0:T(8,128)(2,1)} %rank_in.1, bf16[2,256,1024]{2,1,0:T(8,128)(2,1)} %rank_up.1, ...), custom_call_target="tpu_custom_call" | custom-call | tf_op jit(solution)/shard_map/pallas_call | solution.py:361
  144.5 1.9 %copy.10 = bf16[1024,256]{1,0:T(8,128)(2,1)} copy(bf16[1024,256]{1,0:T(8,128)(2,1)} %shard_map.82) | data formatting | bytes 1048576
where the time goes:
time: 147 us; the launch traced here: 146 us
  Pallas kernels  144 us (98%)
  local copies, waits for them, and re-layouts  1.87 us (1%)
    pallas_call x1, Pallas kernels, per_device(): pl.pallas_call(functools.partial(network, cfg), out_shape=jax.ShapeDtypeS...  144 us

commit v1 on v0

--- a/solution.py
+++ b/solution.py
@@ -9,6 +9,7 @@
 from jax.sharding import PartitionSpec as P
 
 CHUNK_ROWS = 256
+LINE_CHUNK = 128
 SKEW = 1
 LATER = 1
 MESH = pl.DeviceIdType.MESH
@@ -312,6 +313,445 @@
                     spread_copy(u, c, k).wait_send()
 
 
+ORDERS = {
+    (2, 6): (
+        16, 17, 0, 34, 4, 18, 33, 6, 22, 64, 36, 32, 20, 1, 48, 35,
+        49, 2, 19, 54, 70, 81, 118, 86, 51, 3, 65, 102, 97, 80, 96, 21,
+        134, 113, 129, 67, 52, 66, 50, 112, 150, 128, 144, 160, 176, 82, 98, 145,
+        161, 177, 114, 5, 53, 130, 146, 83, 99, 162, 178, 69, 192, 68, 84, 100,
+        37, 208, 224, 240, 272, 85, 193, 256, 115, 131, 209, 116, 132, 194, 320, 147,
+        179, 148, 164, 225, 241, 289, 257, 273, 101, 304, 210, 180, 336, 352, 226, 117,
+        321, 288, 195, 242, 258, 274, 163, 133, 149, 211, 368, 384, 227, 165, 305, 322,
+        212, 196, 400, 243, 275, 291, 259, 181, 337, 353, 306, 228, 290, 244, 292, 197,
+        276, 338, 260, 323, 432, 369, 385, 307, 213, 354, 401, 433, 308, 229, 370, 339,
+        355, 245, 277, 386, 371, 324, 261, 340, 448, 402, 434, 356, 387, 309, 403, 416,
+        372, 388, 404, 449, 464, 341, 293, 435, 325, 357, 436, 450, 466, 373, 389, 480,
+        496, 465, 405, 451, 421, 420, 467, 483, 419, 482, 417, 452, 418, 468, 481, 437,
+        453, 484, 497, 499, 500, 498, 469, 485, 501,
+    ),
+}
+SIZES = {
+    1024: (160, 160, 192, 192, 160, 160),
+}
+
+
+def line_order(layers, chunks):
+    found = ORDERS.get((layers, chunks))
+    if found is not None:
+        return [(code // 16 % 16, code // 256, code % 16) for code in found]
+    groups = [[3, 4], [5], [6], [7, 8, 9, 10], [11], [12, 13], [14], [15]]
+    ticks = [[(step, 0) for step in range(3)]]
+    for l in range(layers):
+        ticks += [[(step, l) for step in group] for group in groups]
+        if l + 1 < layers:
+            ticks[-1] += [(step, l + 1) for step in range(3)]
+    order = []
+    for tick in range(len(ticks) + chunks - 1):
+        for c in range(chunks):
+            if 0 <= tick - c < len(ticks):
+                order += [(step, l, c) for step, l in ticks[tick - c]]
+    at = order.index((2, 0, 0)) + 1
+    order[at:at] = [(0, 0, chunks), (1, 0, chunks)]
+    at = order.index((6, 0, 0)) + 1
+    order[at:at] = [(3, 0, chunks), (4, 0, chunks)]
+    at = order.index((6, 0, min(1, chunks - 1))) + 1
+    order[at:at] = [(5, 0, chunks), (6, 0, chunks), (7, 0, chunks), (8, 0, chunks)]
+    at = order.index((11, 0, 0))
+    order[at:at] = [(9, 0, chunks)]
+    return order
+
+
+def line_network(cfg, tokens, level_bits, up_in, down_in, rank_in, rank_up, rank_down, rank_out, out, *scratch):
+    (xbuf, xrecv, tsend, trecv, terms_to, part, got, full, hid, acc, wup, wdown, outs) = scratch[:13]
+    rest = scratch[13:]
+    layers, rows, width = cfg["layers"], cfg["rows"], cfg["width"]
+    blocks, wb, hb = cfg["blocks"], cfg["wb"], cfg["hb"]
+    n_tok, rank, sizes = cfg["n_tok"], cfg["rank"], cfg["sizes"]
+    chunks = len(sizes)
+    starts = [sum(sizes[:c]) for c in range(chunks)]
+    local_bits = bits_of(blocks)
+    nb = 3
+    levels = local_bits + nb
+    upg, downg = rest[:layers], rest[layers : 2 * layers]
+    wsend, wrecv, wloc, osend, orecv, qsend, qrecv = rest[2 * layers : 2 * layers + 7]
+    xs_sem, xr_sem, ts_sem, tr_sem, as_sem, ar_sem = rest[2 * layers + 7 :]
+
+    me = lax.axis_index("feat")
+    me_tok = lax.axis_index("tok")
+    bit = [(me // (1 << b)) % 2 for b in range(nb)]
+    flip = [(1 << b) * (1 - 2 * bit[b]) for b in range(nb)]
+    across, near, far = [me + flip[b] for b in range(nb)]
+    cross = me + flip[1] + flip[2]
+    is_inner = bit[1] + bit[2] == 1
+    is_outer = bit[1] + bit[2] != 1
+    core_peer = me_tok + 1 - 2 * (me_tok % 2)
+    chip_peer = me_tok + 2 - 4 * ((me_tok // 2) % 2)
+
+    def inner(f):
+        pl.when(is_inner)(f)
+
+    def outer(f):
+        pl.when(is_outer)(f)
+
+    barrier = pltpu.get_barrier_semaphore()
+    for to in (across, near):
+        pl.semaphore_signal(barrier, inc=1, device_id={"feat": to}, device_id_type=MESH)
+    for to in (core_peer, chip_peer):
+        pl.semaphore_signal(barrier, inc=1, device_id={"tok": to}, device_id_type=MESH)
+
+    @inner
+    def _():
+        pl.semaphore_signal(barrier, inc=1, device_id={"feat": cross}, device_id_type=MESH)
+        pl.semaphore_wait(barrier, 5)
+
+    @outer
+    def _():
+        pl.semaphore_wait(barrier, 4)
+
+    def remote(src, dst, send, recv, axis, to):
+        return pltpu.make_async_remote_copy(
+            src_ref=src, dst_ref=dst, send_sem=send, recv_sem=recv, device_id={axis: to}, device_id_type=MESH
+        )
+
+    up_cols, down_cols = up_in.shape[-1], down_in.shape[-2]
+
+    def shard(l, kind, owner):
+        if kind == 0:
+            return upg[l].at[:, :, :, pl.ds(pl.multiple_of(owner * up_cols, up_cols), up_cols)]
+        return downg[l].at[:, :, pl.ds(pl.multiple_of(owner * down_cols, down_cols), down_cols), :]
+
+    def weight_copy(l, kind, way):
+        src = (up_in if kind == 0 else down_in).at[l]
+        if way == 0:
+            return pltpu.make_async_copy(src, shard(l, kind, me_tok), wloc.at[l, kind])
+        if way == 1:
+            to, at = chip_peer, shard(l, kind, me_tok)
+        elif way == 2:
+            to, at = core_peer, shard(l, kind, me_tok)
+        else:
+            src = at = shard(l, kind, chip_peer)
+            to = core_peer
+        return remote(src, at, wsend.at[l, kind, way - 1], wrecv.at[l, kind, way - 1], "tok", to)
+
+    def start_weights(l):
+        for kind in range(2):
+            for way in range(3):
+                weight_copy(l, kind, way).start()
+
+    shared = set()
+
+    def share_weights(l, kind):
+        if (l, kind) in shared:
+            return
+        shared.add((l, kind))
+        weight_copy(l, kind, 1).wait_recv()
+        weight_copy(l, kind, 3).start()
+
+    quarter = rank // n_tok
+
+    def out_rows(slot, owner):
+        at = pl.ds(pl.multiple_of(owner * quarter, quarter), quarter)
+        return outs.at[:, :, at, :] if slot is None else outs.at[slot, :, at, :]
+
+    def share_copy(way):
+        at = out_rows(None, chip_peer if way == 2 else me_tok)
+        return remote(at, at, qsend.at[way], qrecv.at[way], "tok", core_peer if way else chip_peer)
+
+    def share_outs():
+        share_copy(0).wait_recv()
+        share_copy(2).start()
+
+    prepared = set()
+
+    def prepare(l, kind):
+        if (l, kind) in prepared:
+            return
+        prepared.add((l, kind))
+        share_weights(l, kind)
+        weight_copy(l, kind, 0).wait()
+        weight_copy(l, kind, 2).wait_recv()
+        weight_copy(l, kind, 3).wait_recv()
+        order = []
+        for b in range(levels):
+            at = 0
+            for k in range(levels):
+                at = jnp.maximum(at, jnp.where(level_bits[l, k] == b, 1 + k, 0))
+            order.append(at)
+        for j in range(blocks):
+            if kind == 0:
+                wup[l, j, pl.ds(0, wb), :] = upg[l][j, 0]
+                for b in range(levels):
+                    wup[l, j, pl.ds((1 + b) * wb, wb), :] = upg[l][j, order[b]]
+                wup[l, j, pl.ds((1 + levels) * wb, rank), :] = rank_up[l, :, pl.ds(j * hb, hb)]
+            else:
+                wdown[l, j, pl.ds(0, wb), :] = downg[l][j, 0]
+                for b in range(levels):
+                    wdown[l, j, pl.ds((1 + b) * wb, wb), :] = downg[l][j, order[b]]
+
+    def rows_of(c):
+        return pl.ds(starts[c], sizes[c])
+
+    def own_x(l):
+        return xbuf.at[l] if l else tokens
+
+    WAYS = (("own", 0, across), ("own", 1, near), ("own", 3, cross), (1, 2, cross), (3, 2, near), (2, 3, near))
+
+    def x_copy(l, c, way):
+        src, slot, to = WAYS[way]
+        if c == chunks:
+            at = pl.ds(pl.multiple_of(me_tok * quarter, quarter), quarter)
+            src = rank_out.at[:, at, :] if src == "own" else out_rows(src - 1, me_tok)
+            return remote(src, out_rows(slot - 1, me_tok), osend.at[way], orecv.at[slot], "feat", to)
+        at = rows_of(c)
+        src = own_x(l).at[at, :] if src == "own" else xrecv.at[l, src, at, :]
+        return remote(src, xrecv.at[l, slot, at, :], xs_sem.at[l, c, way], xr_sem.at[l, c, slot], "feat", to)
+
+    T_WAYS = ((0, 0, across), (1, 1, near), (2, 2, near), (3, 3, near), (2, 4, cross), (3, 5, cross))
+
+    def t_copy(l, c, way):
+        src, slot, to = T_WAYS[way]
+        at = rows_of(c)
+        return remote(
+            tsend.at[l, src, at, :], trecv.at[l, slot, at, :], ts_sem.at[l, c, way], tr_sem.at[l, c, slot], "feat", to
+        )
+
+    def pair_copy(u, c):
+        at = rows_of(c)
+        return remote(part.at[u, at, :], got.at[u, at, :], as_sem.at[u, c], ar_sem.at[u, c], "feat", across)
+
+    def pair_sum(u, c):
+        pair_copy(u, c).wait_recv()
+        at = rows_of(c)
+        total = part[u, at, :].astype(jnp.float32) + got[u, at, :].astype(jnp.float32)
+        full[u, at, :] = total.astype(jnp.bfloat16)
+
+    def send_cross(l, c):
+        @inner
+        def _():
+            x_copy(l, c, 2).start()
+
+    def send_near(l, c):
+        x_copy(l, c, 1).start()
+
+    def send_across(l, c):
+        x_copy(l, c, 0).start()
+
+    def relay_in(l, c):
+        x_copy(l, c, 1).wait_recv()
+
+        @inner
+        def _():
+            x_copy(l, c, 3).start()
+
+    def relay_cross(l, c):
+        @inner
+        def _():
+            x_copy(l, c, 2).wait_recv()
+            x_copy(l, c, 4).start()
+
+    def relay_out(l, c):
+        @inner
+        def _():
+            x_copy(l, c, 3).wait_recv()
+            x_copy(l, c, 5).start()
+
+    def line_done(l, c):
+        @outer
+        def _():
+            x_copy(l, c, 4).wait_recv()
+            x_copy(l, c, 5).wait_recv()
+
+    def begin(l, c):
+        line_done(l, c)
+        if c == chunks:
+            share_copy(0).start()
+            share_copy(1).start()
+            return
+        at = rows_of(c)
+        total = None
+        for slot, owner in ((0, me), (1, near), (2, far), (3, cross)):
+            x = xrecv[l, slot, at, :] if slot else own_x(l)[at, :]
+            term = jnp.dot(
+                x, rank_in[l, pl.ds(pl.multiple_of(owner * width, width), width), :],
+                preferred_element_type=jnp.float32,
+            )
+            total = term if total is None else total + term
+        part[2 * l, at, :] = total.astype(jnp.bfloat16)
+        pair_copy(2 * l, c).start()
+
+    def latent(l, c):
+        if c == chunks:
+            return share_weights(0, 0)
+        pair_sum(2 * l, c)
+
+    def up(l, c):
+        if c == chunks:
+            return share_weights(0, 1)
+        at = rows_of(c)
+        xin = own_x(l)
+        prepare(l, 0)
+        x_copy(l, c, 0).wait_recv()
+        for j in range(blocks):
+            pieces = [xin[at, pl.ds(j * wb, wb)]]
+            for b in range(local_bits):
+                pieces.append(xin[at, pl.ds((j ^ (1 << b)) * wb, wb)])
+            for b in range(nb):
+                pieces.append(xrecv[l, b, at, pl.ds(j * wb, wb)])
+            pieces.append(full[2 * l, at, :])
+            pre = jnp.dot(
+                jnp.concatenate(pieces, axis=1), wup[l, j], preferred_element_type=jnp.float32
+            )
+            act = 0.5 * pre * (1.0 + lax.erf(pre * (1.0 / math.sqrt(2.0))))
+            hid[at, pl.ds(j * hb, hb)] = act.astype(jnp.bfloat16)
+        part[2 * l + 1, at, :] = jnp.dot(
+            hid[at, :], rank_down[l], preferred_element_type=jnp.float32
+        ).astype(jnp.bfloat16)
+        pair_copy(2 * l + 1, c).start()
+
+    def down(l, c):
+        if c == chunks:
+            return share_outs()
+        at = rows_of(c)
+        xin = own_x(l)
+        prepare(l, 1)
+        own = [None] * blocks
+        for j in range(blocks):
+            col = pl.ds(j * wb, wb)
+            out_j = lax.dot_general(
+                hid[at, pl.ds(j * hb, hb)],
+                wdown[l, j],
+                (((1,), (1,)), ((), ())),
+                preferred_element_type=jnp.float32,
+            )
+            terms = [out_j[:, k * wb : (k + 1) * wb] for k in range(1 + levels)]
+            tsend[l, 0, at, col] = terms[1 + local_bits].astype(jnp.bfloat16)
+            for b in range(1, nb):
+                terms_to[b - 1, at, col] = terms[1 + local_bits + b]
+            for to, value in [(j, terms[0])] + [(j ^ (1 << b), terms[1 + b]) for b in range(local_bits)]:
+                own[to] = value if own[to] is None else own[to] + value
+        for j in range(blocks):
+            col = pl.ds(j * wb, wb)
+            acc[at, col] = own[j] + xin[at, col].astype(jnp.float32)
+
+    def send_t_across(l, c):
+        t_copy(l, c, 0).start()
+
+    outs_ready = set()
+
+    def low_rank(l, c):
+        if not outs_ready:
+            outs_ready.add(0)
+            share_copy(1).wait_recv()
+            share_copy(2).wait_recv()
+        at = rows_of(c)
+        pair_sum(2 * l + 1, c)
+        low = full[2 * l + 1, at, :]
+
+        def term(slot):
+            return jnp.dot(low, outs[slot - 1, l], preferred_element_type=jnp.float32)
+
+        @inner
+        def _():
+            for slot in (1, 2):
+                terms_to[slot - 1, at, :] += term(slot)
+            terms_to[2, at, :] = term(3)
+
+        @outer
+        def _():
+            tsend[l, 3, at, :] = term(3).astype(jnp.bfloat16)
+            t_copy(l, c, 3).start()
+            for slot in (2, 1):
+                tsend[l, slot, at, :] = (terms_to[slot - 1, at, :] + term(slot)).astype(jnp.bfloat16)
+                t_copy(l, c, slot).start()
+
+        acc[at, :] += jnp.dot(low, rank_out[l], preferred_element_type=jnp.float32)
+
+    def pass_on(l, c, slot, way):
+        at = rows_of(c)
+
+        @inner
+        def _():
+            t_copy(l, c, {3: 3, 2: 2, 4: 4}[slot]).wait_recv()
+            src = T_WAYS[way][0]
+            total = terms_to[src - 1, at, :] + trecv[l, slot, at, :].astype(jnp.float32)
+            tsend[l, src, at, :] = total.astype(jnp.bfloat16)
+            t_copy(l, c, way).start()
+
+    def pass_far(l, c):
+        pass_on(l, c, 3, 4)
+
+    def pass_cross(l, c):
+        pass_on(l, c, 2, 5)
+
+    def pass_out(l, c):
+        pass_on(l, c, 4, 1)
+
+    def close(l, c):
+        at = rows_of(c)
+
+        @inner
+        def _():
+            t_copy(l, c, 5).wait_recv()
+            acc[at, :] += trecv[l, 5, at, :].astype(jnp.float32)
+
+        t_copy(l, c, 0).wait_recv()
+        t_copy(l, c, 1).wait_recv()
+        total = acc[at, :]
+        for slot in range(2):
+            total = total + trecv[l, slot, at, :].astype(jnp.float32)
+        result = total.astype(jnp.bfloat16)
+        if l + 1 < layers:
+            xbuf[l + 1, at, :] = result
+        else:
+            out[at, :] = result
+
+    steps = [
+        send_cross, send_near, send_across, relay_in, relay_cross, relay_out, begin, latent, up, down,
+        send_t_across, low_rank, pass_far, pass_cross, pass_out, close,
+    ]
+    weights_left = list(range(layers))
+    for at, (step, l, c) in enumerate(line_order(layers, chunks)):
+        steps[step](l, c)
+        if at == 2:
+            start_weights(weights_left.pop(0))
+        if (step, c) == (9, chunks):
+            while weights_left:
+                start_weights(weights_left.pop(0))
+
+    for l in range(layers):
+        for kind in range(2):
+            for way in range(1, 4):
+                weight_copy(l, kind, way).wait_send()
+        for c in range(chunks + (l == 0)):
+            x_copy(l, c, 1).wait_send()
+
+            @inner
+            def _():
+                for way in range(2, 6):
+                    x_copy(l, c, way).wait_send()
+
+            if c == chunks:
+                continue
+            x_copy(l, c, 0).wait_send()
+            for way in range(2):
+                t_copy(l, c, way).wait_send()
+
+            @inner
+            def _():
+                for way in (4, 5):
+                    t_copy(l, c, way).wait_send()
+
+            @outer
+            def _():
+                for way in (2, 3):
+                    t_copy(l, c, way).wait_send()
+
+            for u in (2 * l, 2 * l + 1):
+                pair_copy(u, c).wait_send()
+    for way in range(3):
+        share_copy(way).wait_send()
+
+
 def per_device(tokens, level_bits, up_blocks, down_blocks, rank_in, rank_up, rank_down, rank_out):
     rows, width = tokens.shape
     layers, blocks, parts, wb, up_cols = up_blocks.shape
@@ -348,18 +788,37 @@
         pltpu.VMEM((layers, blocks, parts * wb, hb), bf16),
     ]
     dma = pltpu.SemaphoreType.DMA
-    if gather:
+    line = gather and nb == 3 and n_tok == 4 and rank % (16 * n_tok) == 0 and rows % LINE_CHUNK == 0
+    if line:
+        sizes = SIZES.get(rows) or (LINE_CHUNK,) * (rows // LINE_CHUNK)
+        cfg["sizes"] = sizes
+        pieces = len(sizes)
+        scratch[1:5] = [
+            pltpu.VMEM((layers, nb + 1, rows, width), bf16),
+            pltpu.VMEM((layers, nb + 1, rows, width), bf16),
+            pltpu.VMEM((layers, 2 * nb, rows, width), bf16),
+            pltpu.VMEM((nb, rows, width), jnp.float32),
+            pltpu.VMEM((uses, rows, rank), bf16),
+        ]
+        scratch[6] = pltpu.VMEM((uses, rows, rank), bf16)
+        scratch += [pltpu.VMEM((nb, layers, rank, width), bf16)]
+        scratch += [pltpu.VMEM((blocks, parts, wb, hb), bf16)] * (2 * layers)
+        scratch += [dma((layers, 2, 3)), dma((layers, 2, 3)), dma((layers, 2)), dma((6,)), dma((4,)), dma((3,)), dma((3,))]
+        scratch += [dma((layers, pieces, 6)), dma((layers, pieces, 4)), dma((layers, pieces, 6)), dma((layers, pieces, 6))]
+        scratch += [dma((uses, pieces))] * 2
+    elif gather:
         scratch += [pltpu.VMEM((blocks, parts, wb, hb), bf16)] * (2 * layers)
         scratch += [
             dma((layers, 2, n_tok - 1)),
             dma((layers, 2, n_tok - 1)),
             dma((layers, 2)),
         ]
-    scratch += [dma((layers, chunks, nb))] * 4 + [dma((uses, chunks, 2 * nb - 1))] * 2
+    if not line:
+        scratch += [dma((layers, chunks, nb))] * 4 + [dma((uses, chunks, 2 * nb - 1))] * 2
     vmem = pl.BlockSpec(memory_space=pltpu.VMEM)
     smem = pl.BlockSpec(memory_space=pltpu.SMEM)
     return pl.pallas_call(
-        functools.partial(network, cfg),
+        functools.partial(line_network if line else network, cfg),
         out_shape=jax.ShapeDtypeStruct((rows, width), bf16),
         in_specs=[vmem, smem] + [vmem] * 6,
         out_specs=vmem,

time: 147 us -> 132 us (0.90)
  Pallas kernels: 144 us -> 130 us
    pallas_call x1, Pallas kernels: 144 us -> 130 us  [per_device(): pl.pallas_call(functools.partial(line_network if line else network, cfg),...]
where the time goes in v1:
time: 132 us
  Pallas kernels  130 us (98%)
  local copies, waits for them, and re-layouts  1.87 us (1%)
    pallas_call x1, Pallas kernels, per_device(): pl.pallas_call(functools.partial(line_network if line else network, cfg),...  130 us

profile of v1, /device:TPU:0, one launch (start us, length us, event | category | flops | bytes accessed | tf_op | source)
XLA Modules:
  0.0 131.9 jit_solution(9491584603462788113)
XLA Ops:
  0.0 130.0 %shard_map.82 = bf16[1024,256]{1,0:T(8,128)(2,1)} custom-call(bf16[1024,256]{1,0:T(8,128)(2,1)} %tokens.1, s32[2,4]{1,0:T(2,128)} %level_bits.1, bf16[2,2,5,128,128]{4,3,2,1,0:T(8,128)(2,1)} %up_in.1, bf16[2,2,5,32,512]{4,3,2,1,0:T(8,128)(2,1)} %bitcast.1, bf16[2,2048,256]{2,1,0:T(8,128)(2,1)} %rank_in.1, bf16[2,256,1024]{2,1,0:T(8,128)(2,1)} %rank_up.1, ...), custom_call_target="tpu_custom_call" | custom-call | tf_op jit(solution)/shard_map/pallas_call | solution.py:820
  130.0 1.9 %copy.10 = bf16[1024,256]{1,0:T(8,128)(2,1)} copy(bf16[1024,256]{1,0:T(8,128)(2,1)} %shard_map.82) | data formatting | bytes 1048576

commit v2 on v1

--- a/solution.py
+++ b/solution.py
@@ -314,24 +314,26 @@
 
 
 ORDERS = {
-    (2, 6): (
-        16, 17, 0, 34, 4, 18, 33, 6, 22, 64, 36, 32, 20, 1, 48, 35,
-        49, 2, 19, 54, 70, 81, 118, 86, 51, 3, 65, 102, 97, 80, 96, 21,
-        134, 113, 129, 67, 52, 66, 50, 112, 150, 128, 144, 160, 176, 82, 98, 145,
-        161, 177, 114, 5, 53, 130, 146, 83, 99, 162, 178, 69, 192, 68, 84, 100,
-        37, 208, 224, 240, 272, 85, 193, 256, 115, 131, 209, 116, 132, 194, 320, 147,
-        179, 148, 164, 225, 241, 289, 257, 273, 101, 304, 210, 180, 336, 352, 226, 117,
-        321, 288, 195, 242, 258, 274, 163, 133, 149, 211, 368, 384, 227, 165, 305, 322,
-        212, 196, 400, 243, 275, 291, 259, 181, 337, 353, 306, 228, 290, 244, 292, 197,
-        276, 338, 260, 323, 432, 369, 385, 307, 213, 354, 401, 433, 308, 229, 370, 339,
-        355, 245, 277, 386, 371, 324, 261, 340, 448, 402, 434, 356, 387, 309, 403, 416,
-        372, 388, 404, 449, 464, 341, 293, 435, 325, 357, 436, 450, 466, 373, 389, 480,
-        496, 465, 405, 451, 421, 420, 467, 483, 419, 482, 417, 452, 418, 468, 481, 437,
-        453, 484, 497, 499, 500, 498, 469, 485, 501,
+    (2, 7): (
+        34, 22, 35, 16, 1, 7, 23, 3, 17, 2, 0, 37, 19, 48, 32, 18,
+        49, 65, 33, 55, 71, 64, 38, 6, 36, 80, 119, 87, 96, 51, 103, 20,
+        81, 97, 50, 66, 112, 135, 128, 54, 113, 129, 21, 151, 82, 98, 4, 144,
+        176, 160, 145, 177, 86, 114, 161, 130, 83, 52, 67, 99, 70, 53, 146, 102,
+        192, 84, 68, 208, 178, 100, 115, 131, 209, 224, 193, 240, 272, 5, 116, 147,
+        163, 132, 179, 256, 85, 162, 225, 241, 273, 257, 210, 69, 101, 148, 289, 194,
+        321, 180, 226, 242, 195, 304, 274, 117, 320, 211, 133, 149, 165, 305, 164, 336,
+        352, 227, 196, 288, 181, 243, 275, 212, 258, 118, 134, 337, 353, 306, 368, 228,
+        259, 290, 244, 292, 322, 276, 150, 166, 182, 197, 213, 260, 338, 369, 385, 384,
+        354, 229, 323, 291, 245, 277, 293, 308, 307, 401, 433, 198, 400, 432, 340, 324,
+        339, 214, 370, 386, 402, 309, 356, 230, 246, 262, 278, 355, 465, 261, 434, 372,
+        388, 326, 404, 416, 449, 325, 371, 387, 436, 310, 294, 341, 450, 481, 357, 342,
+        358, 466, 448, 403, 435, 373, 374, 390, 406, 452, 420, 468, 389, 405, 484, 438,
+        421, 464, 451, 418, 483, 422, 467, 470, 454, 480, 500, 482, 437, 453, 419, 496,
+        417, 486, 469, 502, 485, 499, 498, 497, 501,
     ),
 }
 SIZES = {
-    1024: (160, 160, 192, 192, 160, 160),
+    1024: (128, 128, 160, 160, 160, 160, 128),
 }
 
 
@@ -361,9 +363,10 @@
     return order
 
 
-def line_network(cfg, tokens, level_bits, up_in, down_in, rank_in, rank_up, rank_down, rank_out, out, *scratch):
+def line_network(cfg, tokens, level_bits, up_in, down_in, all_in, all_up, all_down, all_out, out, *scratch):
     (xbuf, xrecv, tsend, trecv, terms_to, part, got, full, hid, acc, wup, wdown, outs) = scratch[:13]
-    rest = scratch[13:]
+    rank_in, rank_down, rank_out, load_sem = scratch[13:17]
+    rest = scratch[17:]
     layers, rows, width = cfg["layers"], cfg["rows"], cfg["width"]
     blocks, wb, hb = cfg["blocks"], cfg["wb"], cfg["hb"]
     n_tok, rank, sizes = cfg["n_tok"], cfg["rank"], cfg["sizes"]
@@ -393,11 +396,35 @@
     def outer(f):
         pl.when(is_outer)(f)
 
+    low = (1 + levels) * wb
+    loads = {"x": [(tokens, xbuf.at[0])], "in": [(all_in, rank_in)]}
+    for l in range(layers):
+        loads["up", l] = [
+            (all_up.at[l, :, pl.ds(j * hb, hb)], wup.at[l, j, pl.ds(low, rank), :]) for j in range(blocks)
+        ]
+    loads["down"] = [(all_down, rank_down)]
+    loads["out"] = [(all_out, rank_out)]
+    pending, count = {}, 0
+    for name, pairs in loads.items():
+        pending[name] = []
+        for src, dst in pairs:
+            pending[name].append(pltpu.make_async_copy(src, dst, load_sem.at[count]))
+            count += 1
+
+    def loaded(*names):
+        for name in names:
+            for copy in pending.pop(name, ()):
+                copy.wait()
+
     barrier = pltpu.get_barrier_semaphore()
     for to in (across, near):
         pl.semaphore_signal(barrier, inc=1, device_id={"feat": to}, device_id_type=MESH)
     for to in (core_peer, chip_peer):
         pl.semaphore_signal(barrier, inc=1, device_id={"tok": to}, device_id_type=MESH)
+
+    for name in pending:
+        for copy in pending[name]:
+            copy.start()
 
     @inner
     def _():
@@ -482,7 +509,6 @@
                 wup[l, j, pl.ds(0, wb), :] = upg[l][j, 0]
                 for b in range(levels):
                     wup[l, j, pl.ds((1 + b) * wb, wb), :] = upg[l][j, order[b]]
-                wup[l, j, pl.ds((1 + levels) * wb, rank), :] = rank_up[l, :, pl.ds(j * hb, hb)]
             else:
                 wdown[l, j, pl.ds(0, wb), :] = downg[l][j, 0]
                 for b in range(levels):
@@ -492,7 +518,7 @@
         return pl.ds(starts[c], sizes[c])
 
     def own_x(l):
-        return xbuf.at[l] if l else tokens
+        return xbuf.at[l]
 
     WAYS = (("own", 0, across), ("own", 1, near), ("own", 3, cross), (1, 2, cross), (3, 2, near), (2, 3, near))
 
@@ -500,10 +526,10 @@
         src, slot, to = WAYS[way]
         if c == chunks:
             at = pl.ds(pl.multiple_of(me_tok * quarter, quarter), quarter)
-            src = rank_out.at[:, at, :] if src == "own" else out_rows(src - 1, me_tok)
+            src = all_out.at[:, at, :] if src == "own" else out_rows(src - 1, me_tok)
             return remote(src, out_rows(slot - 1, me_tok), osend.at[way], orecv.at[slot], "feat", to)
         at = rows_of(c)
-        src = own_x(l).at[at, :] if src == "own" else xrecv.at[l, src, at, :]
+        src = (xbuf.at[l] if l else tokens).at[at, :] if src == "own" else xrecv.at[l, src, at, :]
         return remote(src, xrecv.at[l, slot, at, :], xs_sem.at[l, c, way], xr_sem.at[l, c, slot], "feat", to)
 
     T_WAYS = ((0, 0, across), (1, 1, near), (2, 2, near), (3, 3, near), (2, 4, cross), (3, 5, cross))
@@ -567,6 +593,7 @@
             share_copy(0).start()
             share_copy(1).start()
             return
+        loaded("x", "in")
         at = rows_of(c)
         total = None
         for slot, owner in ((0, me), (1, near), (2, far), (3, cross)):
@@ -590,6 +617,7 @@
         at = rows_of(c)
         xin = own_x(l)
         prepare(l, 0)
+        loaded("down", ("up", l))
         x_copy(l, c, 0).wait_recv()
         for j in range(blocks):
             pieces = [xin[at, pl.ds(j * wb, wb)]]
@@ -641,6 +669,7 @@
     def low_rank(l, c):
         if not outs_ready:
             outs_ready.add(0)
+            loaded("out")
             share_copy(1).wait_recv()
             share_copy(2).wait_recv()
         at = rows_of(c)
@@ -801,7 +830,13 @@
             pltpu.VMEM((uses, rows, rank), bf16),
         ]
         scratch[6] = pltpu.VMEM((uses, rows, rank), bf16)
-        scratch += [pltpu.VMEM((nb, layers, rank, width), bf16)]
+        scratch += [
+            pltpu.VMEM((nb, layers, rank, width), bf16),
+            pltpu.VMEM(rank_in.shape, bf16),
+            pltpu.VMEM(rank_down.shape, bf16),
+            pltpu.VMEM(rank_out.shape, bf16),
+            dma((4 + layers * blocks,)),
+        ]
         scratch += [pltpu.VMEM((blocks, parts, wb, hb), bf16)] * (2 * layers)
         scratch += [dma((layers, 2, 3)), dma((layers, 2, 3)), dma((layers, 2)), dma((6,)), dma((4,)), dma((3,)), dma((3,))]
         scratch += [dma((layers, pieces, 6)), dma((layers, pieces, 4)), dma((layers, pieces, 6)), dma((layers, pieces, 6))]
@@ -817,10 +852,11 @@
         scratch += [dma((layers, chunks, nb))] * 4 + [dma((uses, chunks, 2 * nb - 1))] * 2
     vmem = pl.BlockSpec(memory_space=pltpu.VMEM)
     smem = pl.BlockSpec(memory_space=pltpu.SMEM)
+    held = pl.BlockSpec(memory_space=pl.ANY) if line else vmem
     return pl.pallas_call(
         functools.partial(line_network if line else network, cfg),
         out_shape=jax.ShapeDtypeStruct((rows, width), bf16),
-        in_specs=[vmem, smem] + [vmem] * 6,
+        in_specs=[held, smem] + [held] * 6,
         out_specs=vmem,
         scratch_shapes=scratch,
         compiler_params=pltpu.CompilerParams(

time: 132 us -> 130 us (0.985)
  Pallas kernels: 130 us -> 128 us
    pallas_call x1, Pallas kernels: 130 us -> 128 us  [per_device(): pl.pallas_call(functools.partial(line_network if line else network, cfg),...]
where the time goes in v2:
time: 130 us
  Pallas kernels  128 us (98%)
  local copies, waits for them, and re-layouts  1.87 us (1%)
    pallas_call x1, Pallas kernels, per_device(): pl.pallas_call(functools.partial(line_network if line else network, cfg),...  128 us

profile of v2, /device:TPU:0, one launch (start us, length us, event | category | flops | bytes accessed | tf_op | source)
XLA Modules:
  0.0 129.9 jit_solution(973192467700906256)
XLA Ops:
  0.0 128.0 %shard_map.82 = bf16[1024,256]{1,0:T(8,128)(2,1)} custom-call(bf16[1024,256]{1,0:T(8,128)(2,1)} %tokens.1, s32[2,4]{1,0:T(2,128)} %level_bits.1, bf16[2,2,5,128,128]{4,3,2,1,0:T(8,128)(2,1)} %up_in.1, bf16[2,2,5,32,512]{4,3,2,1,0:T(8,128)(2,1)} %bitcast.1, bf16[2,2048,256]{2,1,0:T(8,128)(2,1)} %all_in.1, bf16[2,256,1024]{2,1,0:T(8,128)(2,1)} %all_up.1, ...), custom_call_target="tpu_custom_call" | custom-call | tf_op jit(solution)/shard_map/pallas_call | solution.py:856
  128.0 1.9 %copy.10 = bf16[1024,256]{1,0:T(8,128)(2,1)} copy(bf16[1024,256]{1,0:T(8,128)(2,1)} %shard_map.82) | data formatting | bytes 1048576

commit v3 on v2

--- a/solution.py
+++ b/solution.py
@@ -315,21 +315,21 @@
 
 ORDERS = {
     (2, 7): (
-        34, 22, 35, 16, 1, 7, 23, 3, 17, 2, 0, 37, 19, 48, 32, 18,
-        49, 65, 33, 55, 71, 64, 38, 6, 36, 80, 119, 87, 96, 51, 103, 20,
-        81, 97, 50, 66, 112, 135, 128, 54, 113, 129, 21, 151, 82, 98, 4, 144,
-        176, 160, 145, 177, 86, 114, 161, 130, 83, 52, 67, 99, 70, 53, 146, 102,
-        192, 84, 68, 208, 178, 100, 115, 131, 209, 224, 193, 240, 272, 5, 116, 147,
-        163, 132, 179, 256, 85, 162, 225, 241, 273, 257, 210, 69, 101, 148, 289, 194,
-        321, 180, 226, 242, 195, 304, 274, 117, 320, 211, 133, 149, 165, 305, 164, 336,
-        352, 227, 196, 288, 181, 243, 275, 212, 258, 118, 134, 337, 353, 306, 368, 228,
-        259, 290, 244, 292, 322, 276, 150, 166, 182, 197, 213, 260, 338, 369, 385, 384,
-        354, 229, 323, 291, 245, 277, 293, 308, 307, 401, 433, 198, 400, 432, 340, 324,
-        339, 214, 370, 386, 402, 309, 356, 230, 246, 262, 278, 355, 465, 261, 434, 372,
-        388, 326, 404, 416, 449, 325, 371, 387, 436, 310, 294, 341, 450, 481, 357, 342,
-        358, 466, 448, 403, 435, 373, 374, 390, 406, 452, 420, 468, 389, 405, 484, 438,
-        421, 464, 451, 418, 483, 422, 467, 470, 454, 480, 500, 482, 437, 453, 419, 496,
-        417, 486, 469, 502, 485, 499, 498, 497, 501,
+        16, 32, 1, 17, 0, 7, 23, 36, 34, 37, 18, 48, 22, 19, 4, 49,
+        55, 71, 54, 80, 64, 2, 50, 33, 65, 81, 51, 119, 87, 96, 103, 97,
+        21, 5, 20, 3, 66, 112, 35, 6, 135, 128, 113, 129, 68, 151, 144, 160,
+        176, 52, 82, 98, 38, 145, 177, 161, 83, 114, 53, 130, 146, 67, 99, 192,
+        162, 70, 208, 84, 178, 100, 224, 86, 193, 240, 115, 131, 209, 288, 272, 256,
+        102, 194, 225, 116, 147, 241, 179, 85, 132, 210, 69, 101, 289, 273, 226, 148,
+        320, 118, 134, 195, 242, 274, 257, 304, 180, 117, 133, 163, 164, 290, 211, 227,
+        305, 149, 181, 258, 150, 243, 275, 337, 196, 291, 336, 352, 212, 321, 353, 322,
+        166, 182, 306, 165, 228, 244, 292, 213, 260, 276, 369, 197, 385, 338, 368, 384,
+        354, 401, 417, 433, 198, 229, 400, 308, 245, 277, 261, 230, 324, 214, 370, 386,
+        416, 340, 259, 402, 418, 246, 294, 307, 449, 356, 278, 432, 323, 293, 434, 325,
+        262, 339, 355, 309, 372, 388, 404, 310, 341, 357, 371, 387, 403, 436, 448, 326,
+        450, 342, 480, 358, 435, 373, 419, 464, 389, 465, 452, 374, 390, 482, 466, 451,
+        481, 406, 467, 420, 468, 484, 438, 496, 405, 421, 437, 422, 454, 483, 498, 453,
+        470, 469, 500, 497, 486, 485, 502, 499, 501,
     ),
 }
 SIZES = {

time: 130 us -> 134 us (1.031)
  Pallas kernels: 128 us -> 132 us
    pallas_call x1, Pallas kernels: 128 us -> 132 us  [per_device(): pl.pallas_call(functools.partial(line_network if line else network, cfg),...]
where the time goes in v3:
time: 134 us
  Pallas kernels  132 us (99%)
  local copies, waits for them, and re-layouts  1.87 us (1%)
    pallas_call x1, Pallas kernels, per_device(): pl.pallas_call(functools.partial(line_network if line else network, cfg),...  132 us

profile of v3, /device:TPU:0, one launch (start us, length us, event | category | flops | bytes accessed | tf_op | source)
XLA Modules:
  0.0 133.7 jit_solution(7543632211104913362)
XLA Ops:
  0.0 131.8 %shard_map.82 = bf16[1024,256]{1,0:T(8,128)(2,1)} custom-call(bf16[1024,256]{1,0:T(8,128)(2,1)} %tokens.1, s32[2,4]{1,0:T(2,128)} %level_bits.1, bf16[2,2,5,128,128]{4,3,2,1,0:T(8,128)(2,1)} %up_in.1, bf16[2,2,5,32,512]{4,3,2,1,0:T(8,128)(2,1)} %bitcast.1, bf16[2,2048,256]{2,1,0:T(8,128)(2,1)} %all_in.1, bf16[2,256,1024]{2,1,0:T(8,128)(2,1)} %all_up.1, ...), custom_call_target="tpu_custom_call" | custom-call | tf_op jit(solution)/shard_map/pallas_call | solution.py:856
  131.8 1.9 %copy.10 = bf16[1024,256]{1,0:T(8,128)(2,1)} copy(bf16[1024,256]{1,0:T(8,128)(2,1)} %shard_map.82) | data formatting | bytes 1048576
